TPU v7x, 32 devices: a whole 2x2x4 slice. The times are simulated.
32 devices in a mesh: grid: 8 (over z, core), vec: 4 (over y, x).
Axes of the slice: x: 2, y: 2, z: 4, core: 2. Of those that a mesh axis runs over, the one named last changes fastest.
Arguments:
- orbitals: bfloat16 [884736, 512], P(('grid', 'vec')), may hold values from -1.296875 to 1.296875
- inverse_panel: bfloat16 [2048, 32], replicated, may hold values from -0.125 to 0.125
- points: int32 [2048], replicated, may hold values from 0 to 884735, as said below
Outputs:
- projected: float32 [2048, 32], P(('grid', 'vec'))
Inputs may be any that keep to these rules, and one draw needn't show every extreme that they name: `points`: distinct cell indices.
All inputs are finite; a program needn't handle non-finite values.
Results may differ from a plain program's by a relative error of at most 0.005.
Values may be sent and summed in bfloat16 or wider, within the bound.
A program may use at most 256 MiB of HBM per device.

v0:
```python
import math
import jax
import jax.numpy as jnp
from jax import lax
from jax.sharding import PartitionSpec as P

NG = 96
SCREEN = 2.25


def wave_tables(count):
    index = lax.iota(jnp.int32, count)
    phase = index[:, None] * index[None, :] % count
    angle = phase.astype(jnp.float32) * (2.0 * math.pi / count)
    return (jnp.cos(angle).astype(jnp.bfloat16), jnp.sin(angle).astype(jnp.bfloat16))


def wavenumber(index, count):
    return jnp.where(index < count // 2, index, index - count).astype(jnp.float32)


def screened(wave_x, wave_y, wave_z):
    squared = (
        wave_x[:, None, None] * wave_x[:, None, None]
        + wave_y[None, :, None] * wave_y[None, :, None]
        + wave_z[None, None, :] * wave_z[None, None, :]
    )
    factor = NG / (2.0 * math.pi) * (NG / (2.0 * math.pi))
    return jnp.where(squared > 0.5, factor / (squared + SCREEN), jnp.float32(0.0))


def mult(data, table, form):
    return jnp.einsum(form, data, table, preferred_element_type=jnp.float32)


def shards(orbitals, inverse_panel, points):
    bf = jnp.bfloat16
    row_count = orbitals.shape[0]
    grid_count = lax.axis_size("grid")
    vec_count = lax.axis_size("vec")
    npoints = points.shape[0]
    offset = (lax.axis_index("grid") * vec_count + lax.axis_index("vec")) * row_count
    local_pos = points - offset
    inside = (local_pos >= 0) & (local_pos < row_count)
    picked = jnp.take(orbitals, jnp.clip(local_pos, 0, row_count - 1), axis=0)
    picked = jnp.where(inside[:, None], picked, jnp.zeros_like(picked)).astype(jnp.float32)
    summed_rows = lax.psum(picked, ("grid", "vec"))
    point_rows = summed_rows.astype(bf)

    def pair_block(block):
        correlation = lax.dot_general(
            block, point_rows, (((1,), (1,)), ((), ())), preferred_element_type=jnp.float32
        )
        return (correlation * correlation).astype(bf)

    pair = lax.map(pair_block, orbitals.reshape(4, row_count // 4, orbitals.shape[1])).reshape(
        row_count, npoints
    )
    fit_cols = lax.dot_general(
        inverse_panel, pair, (((0,), (1,)), ((), ())), preferred_element_type=jnp.float32
    ).astype(bf)
    slab = lax.all_to_all(fit_cols, "vec", split_axis=0, concat_axis=1, tiled=True)
    col_local = slab.shape[0]
    planes = NG // grid_count
    field = slab.reshape(col_local, planes, NG, NG)
    cos_tab, sin_tab = wave_tables(NG)
    z_re = mult(field, cos_tab, "vxyz,zk->vxyk").astype(bf)
    z_im = (-mult(field, sin_tab, "vxyz,zk->vxyk")).astype(bf)
    y_re = (mult(z_re, cos_tab, "vxyz,yk->vxkz") + mult(z_im, sin_tab, "vxyz,yk->vxkz")).astype(bf)
    y_im = (mult(z_im, cos_tab, "vxyz,yk->vxkz") - mult(z_re, sin_tab, "vxyz,yk->vxkz")).astype(bf)
    stacked = jnp.stack([y_re, y_im])
    waves = wavenumber(lax.iota(jnp.int32, NG), NG)
    y_waves = wavenumber(lax.axis_index("grid") * planes + lax.iota(jnp.int32, planes), NG)
    kernel = screened(waves, y_waves, waves)[None]
    piece = lax.all_to_all(stacked, "grid", split_axis=3, concat_axis=2, tiled=True)
    p_re = piece[0]
    p_im = piece[1]
    x_re = mult(p_re, cos_tab, "vxyz,xk->vkyz") + mult(p_im, sin_tab, "vxyz,xk->vkyz")
    x_im = mult(p_im, cos_tab, "vxyz,xk->vkyz") - mult(p_re, sin_tab, "vxyz,xk->vkyz")
    q_re = (x_re * kernel).astype(bf)
    q_im = (x_im * kernel).astype(bf)
    i_re = (mult(q_re, cos_tab, "vxyz,xk->vkyz") - mult(q_im, sin_tab, "vxyz,xk->vkyz")).astype(bf)
    i_im = (mult(q_im, cos_tab, "vxyz,xk->vkyz") + mult(q_re, sin_tab, "vxyz,xk->vkyz")).astype(bf)
    spectrum = lax.all_to_all(
        jnp.stack([i_re, i_im]), "grid", split_axis=2, concat_axis=3, tiled=True
    )
    s_re = spectrum[0]
    s_im = spectrum[1]
    h_re = (mult(s_re, cos_tab, "vxyz,yk->vxkz") - mult(s_im, sin_tab, "vxyz,yk->vxkz")).astype(bf)
    h_im = (mult(s_im, cos_tab, "vxyz,yk->vxkz") + mult(s_re, sin_tab, "vxyz,yk->vxkz")).astype(bf)
    final = mult(h_re, cos_tab, "vxyz,zk->vxyk") - mult(h_im, sin_tab, "vxyz,zk->vxyk")
    potential = (final / float(NG**3)).astype(bf).reshape(col_local, planes * NG * NG)
    pot_rows = lax.all_to_all(potential, "vec", split_axis=1, concat_axis=0, tiled=True)
    scale = 1.0 / math.sqrt(float(NG**3))
    term = lax.dot_general(
        pair, pot_rows, (((0,), (1,)), ((), ())), preferred_element_type=jnp.float32
    )
    partial_block = lax.psum_scatter(
        term * jnp.float32(scale), "grid", scatter_dimension=0, tiled=True
    )
    projected = lax.psum_scatter(partial_block, "vec", scatter_dimension=0, tiled=True)
    return projected


def solution(mesh):
    in_specs = (P(("grid", "vec"), None), P(), P())
    out_specs = P(("grid", "vec"), None)
    return jax.shard_map(shards, mesh=mesh, in_specs=in_specs, out_specs=out_specs, check_vma=False)
```

profile of v0, /device:TPU:0, one launch (start us, length us, event | category | flops | bytes accessed | tf_op | source)
XLA Modules:
  0.0 691.5 jit_solution(2763133241385044677)
XLA Ops:
  8.0 20.3 %gather_fusion = bf16[2048,512]{1,0:T(8,128)(2,1)S(1)} fusion(bf16[27648,512]{1,0:T(8,128)(2,1)} %param.5, s32[2048]{0:T(1024)S(1)} %fusion.73), kind=kCustom, calls=%fused_computation | custom fusion | bytes 4202496 | tf_op jit(solution)/shard_map/jit(_take)/gather | solution.py:45
  28.3 3.4 select_convert_fusion
  31.7 94.7 %all-reduce.1 = bf16[2048,512]{1,0:T(8,128)(2,1)S(1)} all-reduce(f32[2048,512]{1,0:T(8,128)} %select_convert_fusion), channel_id=1, replica_groups=mesh['grid'=8,'vec'=4] {'grid','vec'}, use_global_device_ids=true, to_apply=%region_0.1 | all-reduce | flops 1048576 | bytes 6291456 | tf_op jit(solution)/shard_map/psum | solution.py:47
  126.4 86.1 %while.10 = (s32[]{:T(128)}, bf16[4,6912,2048]{2,1,0:T(8,128)(2,1)}, bf16[4,6912,512]{2,1,0:T(8,128)(2,1)}, bf16[2048,512]{1,0:T(8,128)(2,1)S(1)}, s32[]{:T(128)}) while((s32[]{:T(128)}, bf16[4,6912,2048]{2,1,0:T(8,128)(2,1)}, bf16[4,6912,512]{2,1,0:T(8,128)(2,1)}, bf16[2048,512]{1,0:T(8,128)(2,1)S(1)}, s32[]{:T(128)}) %tuple.28), condition=%wide.region_2.3_spmd, body=%wide.region_1.2_spmd.sunk | while | flops 14523826176 | bytes 37487676 | solution.py:56
  126.4 21.5 %bitcast_dynamic-update-slice_fusion.2 = bf16[4,6912,2048]{2,1,0:T(8,128)(2,1)} fusion(bf16[4,6912,2048]{2,1,0:T(8,128)(2,1)} %get-tuple-element.73, s32[]{:T(128)} %get-tuple-element.72, bf16[2048,512]{1,0:T(8,128)(2,1)S(1)} %get-tuple-element.80, bf16[4,6912,512]{2,1,0:T(8,128)(2,1)} %get-tuple-element.79), kind=kOutput, calls=%fused_computation.2.clone.1 | convolution fusion | flops 14523826176 | bytes 37487616 | tf_op jit(solution)/shard_map/while/body/eval_jaxpr/dot_general | solution.py:51
  147.9 21.5 %bitcast_dynamic-update-slice_fusion.2 = bf16[4,6912,2048]{2,1,0:T(8,128)(2,1)} fusion(bf16[4,6912,2048]{2,1,0:T(8,128)(2,1)} %get-tuple-element.73, s32[]{:T(128)} %get-tuple-element.72, bf16[2048,512]{1,0:T(8,128)(2,1)S(1)} %get-tuple-element.80, bf16[4,6912,512]{2,1,0:T(8,128)(2,1)} %get-tuple-element.79), kind=kOutput, calls=%fused_computation.2.clone.1 | convolution fusion | flops 14523826176 | bytes 37487616 | tf_op jit(solution)/shard_map/while/body/eval_jaxpr/dot_general | solution.py:51
  169.4 21.5 %bitcast_dynamic-update-slice_fusion.2 = bf16[4,6912,2048]{2,1,0:T(8,128)(2,1)} fusion(bf16[4,6912,2048]{2,1,0:T(8,128)(2,1)} %get-tuple-element.73, s32[]{:T(128)} %get-tuple-element.72, bf16[2048,512]{1,0:T(8,128)(2,1)S(1)} %get-tuple-element.80, bf16[4,6912,512]{2,1,0:T(8,128)(2,1)} %get-tuple-element.79), kind=kOutput, calls=%fused_computation.2.clone.1 | convolution fusion | flops 14523826176 | bytes 37487616 | tf_op jit(solution)/shard_map/while/body/eval_jaxpr/dot_general | solution.py:51
  190.9 21.6 %bitcast_dynamic-update-slice_fusion.2 = bf16[4,6912,2048]{2,1,0:T(8,128)(2,1)} fusion(bf16[4,6912,2048]{2,1,0:T(8,128)(2,1)} %get-tuple-element.73, s32[]{:T(128)} %get-tuple-element.72, bf16[2048,512]{1,0:T(8,128)(2,1)S(1)} %get-tuple-element.80, bf16[4,6912,512]{2,1,0:T(8,128)(2,1)} %get-tuple-element.79), kind=kOutput, calls=%fused_computation.2.clone.1 | convolution fusion | flops 14523826176 | bytes 37487616 | tf_op jit(solution)/shard_map/while/body/eval_jaxpr/dot_general | solution.py:51
  212.5 42.6 %fusion.3 = bf16[4,8,27648]{2,1,0:T(8,128)(2,1)S(1)} fusion(bf16[27648,2048]{1,0:T(8,128)(2,1)} %bitcast.3, bf16[2048,32]{0,1:T(8,128)(2,1)S(1)} %copy-done), kind=kOutput, calls=%fused_computation.7 | convolution fusion | flops 3624763392 | bytes 115146752 | tf_op jit(solution)/shard_map/dot_general | solution.py:59
  255.1 23.7 %all_to_all.65 = bf16[4,8,27648]{2,1,0:T(8,128)(2,1)S(1)} all-to-all(bf16[4,8,27648]{2,1,0:T(8,128)(2,1)S(1)} %fusion.3), channel_id=1, replica_groups=mesh['grid'=8,'vec'=4] {'vec'}, dimensions={0} | all-to-all | bytes 3538944 | tf_op jit(solution)/shard_map/all_to_all | solution.py:62
  278.9 2.6 copy.77
  281.5 4.0 reshape.103
  292.5 5.2 copy.82
  297.7 4.6 all-to-all-start.1
  302.9 104.7 %all-to-all-done.1 = bf16[2,8,12,96,96]{4,1,2,0,3:T(8,128)(2,1)} async-done(((bf16[2,8,12,96,96]{4,1,2,0,3:T(8,128)(2,1)}), bf16[2,8,12,96,96]{4,1,2,0,3:T(8,128)(2,1)}, u32[]{:S(2)}, u32[]{:S(2)}) %all-to-all-start.1) | async-done | bytes 3538976 | tf_op jit(solution)/shard_map/all_to_all | solution.py:75
  407.6 3.6 copy.83
  412.2 2.0 fusion.32
  414.4 2.0 fusion.28
  416.4 2.4 fusion.6
  419.8 2.4 fusion.7
  426.5 3.0 copy.98
  429.5 107.7 %all_to_all.66 = bf16[2,8,96,12,96]{4,1,3,0,2:T(8,128)(2,1)S(1)} all-to-all(bf16[2,8,96,12,96]{4,1,3,0,2:T(8,128)(2,1)S(1)} %copy.98), channel_id=1, replica_groups=mesh['grid'=8,'vec'=4] {'grid'}, dimensions={2} | all-to-all | bytes 7077888 | tf_op jit(solution)/shard_map/all_to_all | solution.py:84
  539.1 3.2 fusion.26
  543.9 3.1 fusion.20
  547.1 7.1 %fusion.11 = f32[8,12,96,96]{3,2,1,0:T(8,128)} fusion(f32[96,8,12,96]{3,0,2,1:T(8,128)} %fusion.26, bf16[8,12,96,96]{3,0,2,1:T(8,128)(2,1)} %bitcast.130), kind=kOutput, calls=%fused_computation.27 | convolution fusion | flops 341692416 | bytes 8847360 | tf_op jit(solution)/shard_map/vxyz,zk->vxyk/dot_general | solution.py:33
  554.2 5.9 multiply_convert_fusion.1
  560.1 5.0 all_to_all.57
  565.6 24.6 %all_to_all.67 = bf16[8,4,27648]{2,0,1:T(8,128)(2,1)S(1)} all-to-all(bf16[8,4,27648]{2,0,1:T(8,128)(2,1)S(1)} %copy.110), channel_id=1, replica_groups=mesh['grid'=8,'vec'=4] {'vec'}, dimensions={1} | all-to-all | bytes 3538944 | tf_op jit(solution)/shard_map/all_to_all | solution.py:93
  590.2 38.7 %convolution_multiply_fusion = f32[2048,32]{0,1:T(8,128)} fusion(bf16[27648,2048]{1,0:T(8,128)(2,1)} %bitcast.3, bf16[8,4,27648]{2,0,1:T(8,128)(2,1)S(1)} %all_to_all.67), kind=kOutput, calls=%fused_computation.32 | convolution fusion | flops 3623944192 | bytes 115277824 | tf_op jit(solution)/shard_map/dot_general | solution.py:95
  629.0 28.7 %reduce-scatter.5.cloned.1.call-done = f32[256,32]{0,1:T(8,128)} async-done(((f32[2048,32]{0,1:T(8,128)}), f32[256,32]{0,1:T(8,128)}) %reduce-scatter.5.cloned.1.call-update) | async-done | bytes 32784 | tf_op jit(solution)/shard_map/reduce_scatter | solution.py:98
  657.7 1.5 copy.145
  659.2 23.5 %reduce-scatter.7.cloned.1.call-done = f32[64,32]{1,0:T(8,128)} async-done(((f32[256,32]{1,0:T(8,128)}), f32[64,32]{1,0:T(8,128)}) %reduce-scatter.7.cloned.1.call-update) | async-done | bytes 8208
  (38 shorter events, 21.1 us)
Async XLA Ops:
  6.5 206.0 %copy-start = (bf16[2048,32]{0,1:T(8,128)(2,1)S(1)}, bf16[2048,32]{0,1:T(8,128)(2,1)}, u32[]{:S(2)}) copy-start(bf16[2048,32]{0,1:T(8,128)(2,1)} %param.6) | copy-start | bytes 393220
  297.7 109.8 %all-to-all-start.1 = ((bf16[2,8,12,96,96]{4,1,2,0,3:T(8,128)(2,1)}), bf16[2,8,12,96,96]{4,1,2,0,3:T(8,128)(2,1)}, u32[]{:S(2)}, u32[]{:S(2)}) async-start(bf16[2,8,12,96,96]{4,1,2,0,3:T(8,128)(2,1)} %copy.82), calls=%async_computation.1 | async-start | bytes 9437184 | tf_op jit(solution)/shard_map/all_to_all | solution.py:75
  302.3 355.4 %reduce-scatter.5.cloned.1.call-start = ((), (), s32[]{:S(2)}) async-start(), calls=%async_computation.6 | async-start | bytes 294912 | tf_op jit(solution)/shard_map/reduce_scatter | solution.py:98
  542.5 1.4 copy-start.2
  590.2 94.0 %copy-start.1 = (bf16[2048,32]{0,1:T(8,128)(2,1)S(1)}, bf16[2048,32]{0,1:T(8,128)(2,1)}, u32[]{:S(2)}) copy-start(bf16[2048,32]{0,1:T(8,128)(2,1)} %param.6) | copy-start | bytes 393220
  628.9 53.8 %reduce-scatter.7.cloned.1.call-start = ((), (), s32[]{:S(2)}) async-start(), calls=%async_computation.7 | async-start | bytes 163840
Sparse Core Ops, SparseCore 0:
  629.1 28.6 reduce-scatter.4
  660.5 22.2 reduce-scatter.6
where the time goes:
time: 697 us; the launch traced here: 691 us
  blocking collectives  251 us (36%)
  matrix products  206 us (30%)
  waiting for transfers between devices  157 us (23%)
  local copies, waits for them, and re-layouts  51.9 us (7%)
  between operations  14.1 us (2%)
  other arithmetic  7.31 us (1%)
    all_to_all x1, blocking collectives, shards(): lax.all_to_all(jnp.stack([i_re, i_im]), 'grid', split_axis=2, concat_axis...  108 us
    all_to_all x1, waiting for transfers between devices, shards(): lax.all_to_all(stacked, 'grid', split_axis=3, concat_axis=2, tiled=True)  105 us
    psum x1, blocking collectives, shards(): summed_rows = lax.psum(picked, ('grid', 'vec'))  94.7 us
    dot_general x4, matrix products, pair_block(): lax.dot_general(block, point_rows, (((1,), (1,)), ((), ())), preferred_el...  86.1 us
    dot_general x1, matrix products, shards(): lax.dot_general(inverse_panel, pair, (((0,), (1,)), ((), ())), preferred_...  42.6 us
    dot_general x1, matrix products, shards(): lax.dot_general(pair, pot_rows, (((0,), (1,)), ((), ())), preferred_eleme...  38.7 us
    dot_general x18, matrix products, mult(): return jnp.einsum(form, data, table, preferred_element_type=jnp.float32)  38.2 us
    reduce_scatter x1, waiting for transfers between devices, shards(): lax.psum_scatter(term * jnp.float32(scale), 'grid', scatter_dimension=0,...  28.7 us
  transfers between devices with their start and end apart: 3, of which 3 were waited for; matrix products, arithmetic and copies ran while one was open for 0% of the time, Pallas kernels for 0%

commit v1 on v0

--- a/solution.py
+++ b/solution.py
@@ -44,7 +44,7 @@
     inside = (local_pos >= 0) & (local_pos < row_count)
     picked = jnp.take(orbitals, jnp.clip(local_pos, 0, row_count - 1), axis=0)
     picked = jnp.where(inside[:, None], picked, jnp.zeros_like(picked)).astype(jnp.float32)
-    summed_rows = lax.psum(picked, ("grid", "vec"))
+    summed_rows = lax.psum(lax.psum(picked, "vec"), "grid")
     point_rows = summed_rows.astype(bf)
 
     def pair_block(block):

time: 697 us -> 800 us (1.15)
  waiting for transfers between devices: 157 us -> 255 us
  starting transfers between devices: 4.87 us -> 14.7 us
  blocking collectives: 251 us -> 243 us
    psum x0 -> x1, waiting for transfers between devices: none -> 106 us  [shards(): summed_rows = lax.psum(lax.psum(picked, 'vec'), 'grid')]
    reduce_scatter x1, starting transfers between devices: 0.21 us -> 8.78 us  [shards(): lax.psum_scatter(term * jnp.float32(scale), 'grid', scatter_dimension=0,...]
    all_to_all x1, waiting for transfers between devices: 105 us -> 96.2 us  [shards(): lax.all_to_all(stacked, 'grid', split_axis=3, concat_axis=2, tiled=True)]
    unnamed x3 -> x4, waiting for transfers between devices: 23.6 us -> 23.7 us
  transfers between devices with their start and end apart: 3 -> 4, of which waited for: 3 -> 4; matrix products, arithmetic and copies ran while one was open for 0% -> 0% of each run, Pallas kernels for 0% -> 0%
where the time goes in v1:
time: 800 us; the launch traced here: 791 us
  waiting for transfers between devices  255 us (32%)
  blocking collectives  243 us (30%)
  matrix products  206 us (26%)
  local copies, waits for them, and re-layouts  51.5 us (6%)
  starting transfers between devices  14.7 us (2%)
  between operations  13.8 us (2%)
    all_to_all x1, blocking collectives, shards(): lax.all_to_all(jnp.stack([i_re, i_im]), 'grid', split_axis=2, concat_axis...  108 us
    psum x1, waiting for transfers between devices, shards(): summed_rows = lax.psum(lax.psum(picked, 'vec'), 'grid')  106 us
    all_to_all x1, waiting for transfers between devices, shards(): lax.all_to_all(stacked, 'grid', split_axis=3, concat_axis=2, tiled=True)  96.2 us
    psum x1, blocking collectives, shards(): summed_rows = lax.psum(lax.psum(picked, 'vec'), 'grid')  88.9 us
    dot_general x4, matrix products, pair_block(): lax.dot_general(block, point_rows, (((1,), (1,)), ((), ())), preferred_el...  86.1 us
    dot_general x1, matrix products, shards(): lax.dot_general(inverse_panel, pair, (((0,), (1,)), ((), ())), preferred_...  42.6 us
    dot_general x1, matrix products, shards(): lax.dot_general(pair, pot_rows, (((0,), (1,)), ((), ())), preferred_eleme...  38.7 us
    dot_general x18, matrix products, mult(): return jnp.einsum(form, data, table, preferred_element_type=jnp.float32)  38.2 us
  transfers between devices with their start and end apart: 4, of which 4 were waited for; matrix products, arithmetic and copies ran while one was open for 0% of the time, Pallas kernels for 0%

profile of v1, /device:TPU:0, one launch (start us, length us, event | category | flops | bytes accessed | tf_op | source)
XLA Modules:
  0.0 790.9 jit_solution(69470794796828960)
XLA Ops:
  8.0 20.3 %gather_fusion = bf16[2048,512]{1,0:T(8,128)(2,1)S(1)} fusion(bf16[27648,512]{1,0:T(8,128)(2,1)} %param.5, s32[2048]{0:T(1024)S(1)} %fusion.73), kind=kCustom, calls=%fused_computation | custom fusion | bytes 4202496 | tf_op jit(solution)/shard_map/jit(_take)/gather | solution.py:45
  28.3 3.5 select_convert_fusion
  31.8 106.5 %all-reduce.3.cloned.1.call-done = f32[2048,512]{1,0:T(8,128)} async-done(((f32[2048,512]{1,0:T(8,128)}), f32[2048,512]{1,0:T(8,128)}) %all-reduce.3.cloned.1.call-update) | async-done | bytes 4194320 | tf_op jit(solution)/shard_map/psum | solution.py:47
  138.2 88.9 %all-reduce.4 = bf16[2048,512]{1,0:T(8,128)(2,1)S(1)} all-reduce(f32[2048,512]{1,0:T(8,128)} %all-reduce.3.cloned.1.call-done), channel_id=1, replica_groups=mesh['grid'=8,'vec'=4] {'grid'}, use_global_device_ids=true, to_apply=%region_1.2 | all-reduce | flops 1048576 | bytes 6291456 | tf_op jit(solution)/shard_map/psum | solution.py:47
  227.1 86.1 %while.10 = (s32[]{:T(128)}, bf16[4,6912,2048]{2,1,0:T(8,128)(2,1)}, bf16[4,6912,512]{2,1,0:T(8,128)(2,1)}, bf16[2048,512]{1,0:T(8,128)(2,1)S(1)}, s32[]{:T(128)}) while((s32[]{:T(128)}, bf16[4,6912,2048]{2,1,0:T(8,128)(2,1)}, bf16[4,6912,512]{2,1,0:T(8,128)(2,1)}, bf16[2048,512]{1,0:T(8,128)(2,1)S(1)}, s32[]{:T(128)}) %tuple.30), condition=%wide.region_3.4_spmd, body=%wide.region_2.3_spmd.sunk | while | flops 14523826176 | bytes 37487676 | solution.py:56
  227.1 21.5 %bitcast_dynamic-update-slice_fusion.2 = bf16[4,6912,2048]{2,1,0:T(8,128)(2,1)} fusion(bf16[4,6912,2048]{2,1,0:T(8,128)(2,1)} %get-tuple-element.73, s32[]{:T(128)} %get-tuple-element.72, bf16[2048,512]{1,0:T(8,128)(2,1)S(1)} %get-tuple-element.80, bf16[4,6912,512]{2,1,0:T(8,128)(2,1)} %get-tuple-element.79), kind=kOutput, calls=%fused_computation.2.clone.1 | convolution fusion | flops 14523826176 | bytes 37487616 | tf_op jit(solution)/shard_map/while/body/eval_jaxpr/dot_general | solution.py:51
  248.6 21.4 %bitcast_dynamic-update-slice_fusion.2 = bf16[4,6912,2048]{2,1,0:T(8,128)(2,1)} fusion(bf16[4,6912,2048]{2,1,0:T(8,128)(2,1)} %get-tuple-element.73, s32[]{:T(128)} %get-tuple-element.72, bf16[2048,512]{1,0:T(8,128)(2,1)S(1)} %get-tuple-element.80, bf16[4,6912,512]{2,1,0:T(8,128)(2,1)} %get-tuple-element.79), kind=kOutput, calls=%fused_computation.2.clone.1 | convolution fusion | flops 14523826176 | bytes 37487616 | tf_op jit(solution)/shard_map/while/body/eval_jaxpr/dot_general | solution.py:51
  270.1 21.5 %bitcast_dynamic-update-slice_fusion.2 = bf16[4,6912,2048]{2,1,0:T(8,128)(2,1)} fusion(bf16[4,6912,2048]{2,1,0:T(8,128)(2,1)} %get-tuple-element.73, s32[]{:T(128)} %get-tuple-element.72, bf16[2048,512]{1,0:T(8,128)(2,1)S(1)} %get-tuple-element.80, bf16[4,6912,512]{2,1,0:T(8,128)(2,1)} %get-tuple-element.79), kind=kOutput, calls=%fused_computation.2.clone.1 | convolution fusion | flops 14523826176 | bytes 37487616 | tf_op jit(solution)/shard_map/while/body/eval_jaxpr/dot_general | solution.py:51
  291.6 21.6 %bitcast_dynamic-update-slice_fusion.2 = bf16[4,6912,2048]{2,1,0:T(8,128)(2,1)} fusion(bf16[4,6912,2048]{2,1,0:T(8,128)(2,1)} %get-tuple-element.73, s32[]{:T(128)} %get-tuple-element.72, bf16[2048,512]{1,0:T(8,128)(2,1)S(1)} %get-tuple-element.80, bf16[4,6912,512]{2,1,0:T(8,128)(2,1)} %get-tuple-element.79), kind=kOutput, calls=%fused_computation.2.clone.1 | convolution fusion | flops 14523826176 | bytes 37487616 | tf_op jit(solution)/shard_map/while/body/eval_jaxpr/dot_general | solution.py:51
  313.2 42.6 %fusion.3 = bf16[4,8,27648]{2,1,0:T(8,128)(2,1)S(1)} fusion(bf16[27648,2048]{1,0:T(8,128)(2,1)} %bitcast.3, bf16[2048,32]{0,1:T(8,128)(2,1)S(1)} %copy-done), kind=kOutput, calls=%fused_computation.7 | convolution fusion | flops 3624763392 | bytes 115146752 | tf_op jit(solution)/shard_map/dot_general | solution.py:59
  355.9 21.6 %all_to_all.65 = bf16[4,8,27648]{2,1,0:T(8,128)(2,1)S(1)} all-to-all(bf16[4,8,27648]{2,1,0:T(8,128)(2,1)S(1)} %fusion.3), channel_id=1, replica_groups=mesh['grid'=8,'vec'=4] {'vec'}, dimensions={0} | all-to-all | bytes 3538944 | tf_op jit(solution)/shard_map/all_to_all | solution.py:62
  377.5 2.6 copy.77
  380.1 3.6 reshape.103
  390.7 5.2 copy.82
  395.9 5.9 all-to-all-start.1
  401.8 8.8 %reduce-scatter.5.cloned.1.call-start = ((), (), s32[]{:S(2)}) async-start(), calls=%async_computation.7 | async-start | bytes 294912 | tf_op jit(solution)/shard_map/reduce_scatter | solution.py:98
  410.9 96.2 %all-to-all-done.1 = bf16[2,8,12,96,96]{4,1,2,0,3:T(8,128)(2,1)} async-done(((bf16[2,8,12,96,96]{4,1,2,0,3:T(8,128)(2,1)}), bf16[2,8,12,96,96]{4,1,2,0,3:T(8,128)(2,1)}, u32[]{:S(2)}, u32[]{:S(2)}) %all-to-all-start.1) | async-done | bytes 3538976 | tf_op jit(solution)/shard_map/all_to_all | solution.py:75
  507.1 3.6 copy.83
  514.0 2.0 fusion.28
  515.9 2.4 fusion.6
  519.3 2.4 fusion.7
  526.0 3.0 copy.98
  529.1 107.7 %all_to_all.66 = bf16[2,8,96,12,96]{4,1,3,0,2:T(8,128)(2,1)S(1)} all-to-all(bf16[2,8,96,12,96]{4,1,3,0,2:T(8,128)(2,1)S(1)} %copy.98), channel_id=1, replica_groups=mesh['grid'=8,'vec'=4] {'grid'}, dimensions={2} | all-to-all | bytes 7077888 | tf_op jit(solution)/shard_map/all_to_all | solution.py:84
  638.7 3.2 fusion.26
  643.5 3.1 fusion.20
  646.6 7.1 fusion.11
  653.7 5.9 multiply_convert_fusion.1
  659.6 5.0 all_to_all.57
  665.1 24.6 %all_to_all.67 = bf16[8,4,27648]{2,0,1:T(8,128)(2,1)S(1)} all-to-all(bf16[8,4,27648]{2,0,1:T(8,128)(2,1)S(1)} %copy.110), channel_id=1, replica_groups=mesh['grid'=8,'vec'=4] {'vec'}, dimensions={1} | all-to-all | bytes 3538944 | tf_op jit(solution)/shard_map/all_to_all | solution.py:93
  689.8 38.7 %convolution_multiply_fusion = f32[2048,32]{0,1:T(8,128)} fusion(bf16[27648,2048]{1,0:T(8,128)(2,1)} %bitcast.3, bf16[8,4,27648]{2,0,1:T(8,128)(2,1)S(1)} %all_to_all.67), kind=kOutput, calls=%fused_computation.32 | convolution fusion | flops 3623944192 | bytes 115277824 | tf_op jit(solution)/shard_map/dot_general | solution.py:95
  728.5 28.8 %reduce-scatter.5.cloned.1.call-done = f32[256,32]{0,1:T(8,128)} async-done(((f32[2048,32]{0,1:T(8,128)}), f32[256,32]{0,1:T(8,128)}) %reduce-scatter.5.cloned.1.call-update) | async-done | bytes 32784 | tf_op jit(solution)/shard_map/reduce_scatter | solution.py:98
  758.8 23.6 %reduce-scatter.7.cloned.1.call-done = f32[64,32]{1,0:T(8,128)} async-done(((f32[256,32]{1,0:T(8,128)}), f32[64,32]{1,0:T(8,128)}) %reduce-scatter.7.cloned.1.call-update) | async-done | bytes 8208
  (41 shorter events, 24.3 us)
Async XLA Ops:
  6.5 306.7 %copy-start = (bf16[2048,32]{0,1:T(8,128)(2,1)S(1)}, bf16[2048,32]{0,1:T(8,128)(2,1)}, u32[]{:S(2)}) copy-start(bf16[2048,32]{0,1:T(8,128)(2,1)} %param.6) | copy-start | bytes 393220
  6.5 131.7 %all-reduce.3.cloned.1.call-start = ((), (), s32[]{:S(2)}) async-start(), calls=%async_computation.6 | async-start | bytes 8388608 | tf_op jit(solution)/shard_map/psum | solution.py:47
  395.9 111.2 %all-to-all-start.1 = ((bf16[2,8,12,96,96]{4,1,2,0,3:T(8,128)(2,1)}), bf16[2,8,12,96,96]{4,1,2,0,3:T(8,128)(2,1)}, u32[]{:S(2)}, u32[]{:S(2)}) async-start(bf16[2,8,12,96,96]{4,1,2,0,3:T(8,128)(2,1)} %copy.82), calls=%async_computation.1 | async-start | bytes 9437184 | tf_op jit(solution)/shard_map/all_to_all | solution.py:75
  401.8 355.5 %reduce-scatter.5.cloned.1.call-start = ((), (), s32[]{:S(2)}) async-start(), calls=%async_computation.7 | async-start | bytes 294912 | tf_op jit(solution)/shard_map/reduce_scatter | solution.py:98
  642.1 1.4 copy-start.2
  689.8 94.1 %copy-start.1 = (bf16[2048,32]{0,1:T(8,128)(2,1)S(1)}, bf16[2048,32]{0,1:T(8,128)(2,1)}, u32[]{:S(2)}) copy-start(bf16[2048,32]{0,1:T(8,128)(2,1)} %param.6) | copy-start | bytes 393220
  728.5 54.0 %reduce-scatter.7.cloned.1.call-start = ((), (), s32[]{:S(2)}) async-start(), calls=%async_computation.8 | async-start | bytes 163840
Sparse Core Ops, SparseCore 0:
  31.9 106.3 all-reduce.2
  728.6 28.6 reduce-scatter.4
  760.0 22.3 reduce-scatter.6
